TPU v7x, 256 devices: a whole 4x4x8 slice. The times are simulated.
256 devices in a mesh: lat: 16 (over y, x), kpt: 16 (over z, core).
Axes of the slice: x: 4, y: 4, z: 8, core: 2. Of those that a mesh axis runs over, the one named last changes fastest.
Arguments:
- coarse: bfloat16 [2, 16, 256, 12288], P(None, 'lat', 'kpt'), may hold values from -0.1875 to 0.1875
- rp_vectors: int32 [16, 3], P('lat'), may hold values from -4 to 4
- rp_weights: int32 [16], P('lat'), may hold values from 1 to 3
- re_vectors: int32 [256, 3], replicated, may hold values from -4 to 4
- re_weights: int32 [256], replicated, may hold values from 1 to 3
- q_points: float32 [2, 3], replicated, may hold values from 0 to 1
- k_points: float32 [1024, 3], P('kpt'), may hold values from 0 to 1
- modes_rot: bfloat16 [2, 2, 48, 48], replicated, may hold values from -0.625 to 0.625
- u_k: bfloat16 [2, 1024, 16, 16], P(None, 'kpt'), may hold values from -1 to 1
- u_kq: bfloat16 [2, 2, 1024, 16, 16], P(None, None, 'kpt'), may hold values from -1 to 1
- mask_k: int32 [1024, 16], P('kpt'), may hold values 0 or 1
- mask_kq: int32 [2, 1024, 16], P(None, 'kpt'), may hold values 0 or 1
Outputs:
- coupling: bfloat16 [2, 1024, 2, 12288], P(None, 'kpt', None, 'lat')
All inputs are finite; a program needn't handle non-finite values. No bound on the sum of `mask_k` or of `mask_kq` on one device may be relied on, other than what follows from the above.
Results may differ from a plain program's by a relative error of at most 0.017.
Values may be sent and summed in bfloat16 or wider, within the bound.
No kernel may reach another device: no remote copies, remote signals or barrier semaphores. Data moves between devices by JAX's collectives and lax.ppermute only.
A program may use at most 64 MiB of HBM per device.

v0:
```python
import jax
import jax.numpy as jnp
from jax import lax
from jax.sharding import PartitionSpec as P

two_pi = 6.283185307179586


def phases(points, vectors, weights):
    cells = vectors.astype(jnp.float32)
    argument = two_pi * (
        points[:, 0:1] * cells[None, :, 0]
        + points[:, 1:2] * cells[None, :, 1]
        + points[:, 2:3] * cells[None, :, 2]
    )
    inverse = 1.0 / weights.astype(jnp.float32)
    return (
        (jnp.cos(argument) * inverse).astype(jnp.bfloat16),
        (jnp.sin(argument) * inverse).astype(jnp.bfloat16),
    )


def rotate_modes(values, modes_rot):
    shape = values.shape
    mode_count = modes_rot.shape[2]
    split = values.reshape(shape[0], shape[1], shape[2], mode_count, shape[3] // mode_count)
    br = jnp.einsum(
        "qmn,qrmx->qrnx", modes_rot[0], split[0], preferred_element_type=jnp.float32
    ) - jnp.einsum("qmn,qrmx->qrnx", modes_rot[1], split[1], preferred_element_type=jnp.float32)
    bi = jnp.einsum(
        "qmn,qrmx->qrnx", modes_rot[0], split[1], preferred_element_type=jnp.float32
    ) + jnp.einsum("qmn,qrmx->qrnx", modes_rot[1], split[0], preferred_element_type=jnp.float32)
    return jnp.stack([br, bi]).reshape(shape).astype(jnp.bfloat16)


def phonon_sum(block, vectors, weights, q_points):
    phase_real, phase_imag = phases(q_points, vectors, weights)
    rows = block.shape[1]
    cells = block.shape[2]
    lanes = block.shape[3]
    flat_real = block[0].reshape(rows, cells * lanes)
    flat_imag = block[1].reshape(rows, cells * lanes)
    part_real = jnp.dot(phase_real, flat_real, preferred_element_type=jnp.float32) - jnp.dot(
        phase_imag, flat_imag, preferred_element_type=jnp.float32
    )
    part_imag = jnp.dot(phase_real, flat_imag, preferred_element_type=jnp.float32) + jnp.dot(
        phase_imag, flat_real, preferred_element_type=jnp.float32
    )
    return jnp.stack([part_real, part_imag]).reshape(2, q_points.shape[0], cells, lanes)


def per_device(
    coarse,
    rp_vectors,
    rp_weights,
    re_vectors,
    re_weights,
    q_points,
    k_points,
    modes_rot,
    u_k,
    u_kq,
    mask_k,
    mask_kq,
):
    q_count = q_points.shape[0]
    k_count = k_points.shape[0]
    band_count = u_k.shape[2]
    partial_value = phonon_sum(coarse, rp_vectors, rp_weights, q_points)
    summed = lax.psum_scatter(partial_value, "lat", scatter_dimension=2, tiled=True).astype(
        jnp.bfloat16
    )
    rotated = rotate_modes(summed, modes_rot)
    shared = lax.all_to_all(rotated, "lat", split_axis=3, concat_axis=2, tiled=True)
    lane_local = shared.shape[3]
    portion = lax.all_gather(shared, "kpt", axis=2, tiled=True)
    kreal, kimag = phases(k_points, re_vectors, re_weights)
    er = jnp.einsum(
        "kr,qrx->kqx", kreal, portion[0], preferred_element_type=jnp.float32
    ) - jnp.einsum("kr,qrx->kqx", kimag, portion[1], preferred_element_type=jnp.float32)
    ei = jnp.einsum(
        "kr,qrx->kqx", kreal, portion[1], preferred_element_type=jnp.float32
    ) + jnp.einsum("kr,qrx->kqx", kimag, portion[0], preferred_element_type=jnp.float32)
    totals = jnp.stack([er, ei])
    mode_local = lane_local // (band_count * band_count)
    field = totals.astype(jnp.bfloat16).reshape(
        2, k_count, q_count, mode_local, band_count, band_count
    )
    tr = jnp.einsum(
        "kqmab,kbn->kqman", field[0], u_k[0], preferred_element_type=jnp.float32
    ) - jnp.einsum("kqmab,kbn->kqman", field[1], u_k[1], preferred_element_type=jnp.float32)
    ti = jnp.einsum(
        "kqmab,kbn->kqman", field[0], u_k[1], preferred_element_type=jnp.float32
    ) + jnp.einsum("kqmab,kbn->kqman", field[1], u_k[0], preferred_element_type=jnp.float32)
    tr = tr.astype(jnp.bfloat16)
    ti = ti.astype(jnp.bfloat16)
    outr = jnp.einsum(
        "qkac,kqman->kqmcn", u_kq[0], tr, preferred_element_type=jnp.float32
    ) + jnp.einsum("qkac,kqman->kqmcn", u_kq[1], ti, preferred_element_type=jnp.float32)
    outi = jnp.einsum(
        "qkac,kqman->kqmcn", u_kq[0], ti, preferred_element_type=jnp.float32
    ) - jnp.einsum("qkac,kqman->kqmcn", u_kq[1], tr, preferred_element_type=jnp.float32)
    window = (
        jnp.transpose(mask_kq.astype(jnp.float32), (1, 0, 2))[:, :, None, :, None]
        * mask_k.astype(jnp.float32)[:, None, None, None, :]
    )
    result = jnp.stack([outr * window, outi * window])
    return result.reshape(2, k_count, q_count, lane_local).astype(jnp.bfloat16)


def solution(mesh):
    placed = (
        P(None, "lat", "kpt", None),
        P("lat", None),
        P("lat"),
        P(),
        P(),
        P(),
        P("kpt", None),
        P(),
        P(None, "kpt", None, None),
        P(None, None, "kpt", None, None),
        P("kpt", None),
        P(None, "kpt", None),
    )
    return jax.shard_map(
        per_device,
        mesh=mesh,
        in_specs=placed,
        out_specs=P(None, "kpt", None, "lat"),
        check_vma=False,
    )
```

profile of v0, /device:TPU:1, one launch (start us, length us, event | category | flops | bytes accessed | tf_op | source)
XLA Modules:
  0.0 256.3 jit_solution(5092199044945277099)
XLA Ops:
  6.5 0.0 all-gather.2.cloned.1.call-start
  7.2 0.7 convert_element_type.53
  7.8 0.6 fusion.56
  8.5 1.2 convert_bitcast_fusion.1
  9.7 0.0 copy-start.10
  9.7 0.2 copy.137
  9.9 0.2 copy.138
  10.1 0.3 copy-done.10
  10.4 2.1 convert_reduce_fusion.1
  12.4 1.5 multiply_subtract_fusion
  13.9 1.4 pad_maximum_fusion
  15.3 0.0 copy-start.15
  15.4 0.0 copy-start.7
  15.4 86.5 %all-reduce.2 = bf16[2,2,16,12288]{3,1,2,0:T(2,128)(2,1)} all-reduce(f32[2,2,16,12288]{3,1,2,0:T(2,128)S(1)} %pad_maximum_fusion), channel_id=2, replica_groups=mesh['lat'=16,'kpt'=16] {'lat'}, use_global_device_ids=true, to_apply=%region_0.0.clone | all-reduce | flops 786432 | bytes 4718592
  101.9 0.0 copy-done.15
  101.9 0.6 dynamic-slice
  102.5 1.6 dynamic-slice_convert_fusion
  104.1 0.1 fusion.54
  104.2 0.0 copy-done.7
  104.2 0.2 fusion.25
  104.4 0.2 fusion.27
  104.6 0.2 fusion.4
  104.8 0.2 fusion.5
  105.0 0.1 pad_maximum_fusion.2
  105.1 10.0 %copy.99 = bf16[2,2,1,12288]{1,0,2,3:T(2,128)(2,1)} copy(bf16[2,2,1,12288]{3,1,2,0:T(2,128)(2,1)S(1)} %pad_maximum_fusion.2) | data formatting | bytes 196608 | tf_op jit(solution)/shard_map/stack | solution.py:33
  115.1 13.7 %reshape.158 = bf16[16,2,1536]{2,1,0:T(2,128)(2,1)S(1)} reshape(bf16[12288,1,2,2]{3,2,1,0:T(2,128)(2,1)} %bitcast.147) | data formatting | bytes 196608
  128.8 9.2 %all_to_all.12 = bf16[16,2,1536]{2,1,0:T(2,128)(2,1)S(1)} all-to-all(bf16[16,2,1536]{2,1,0:T(2,128)(2,1)S(1)} %reshape.158), channel_id=1, replica_groups=mesh['lat'=16,'kpt'=16] {'lat'}, dimensions={0} | all-to-all | bytes 196608 | tf_op jit(solution)/shard_map/all_to_all | solution.py:74
  138.0 14.7 %reshape.159 = bf16[12288,1,2,2]{3,2,1,0:T(2,128)(2,1)} reshape(bf16[16,2,1536]{2,1,0:T(2,128)(2,1)S(1)} %all_to_all.12) | data formatting | bytes 196608
  152.8 9.9 %copy.128 = bf16[2,2,16,768]{3,2,1,0:T(8,128)(2,1)} copy(bf16[2,2,16,768]{1,0,3,2:T(2,128)(2,1)} %bitcast.148) | data formatting | bytes 196608 | tf_op jit(solution)/shard_map/all_to_all | solution.py:74
  162.7 0.0 all-gather.2.cloned.1.call-update
  162.7 0.0 copy-done.12
  162.7 0.0 copy-done.11
  162.7 0.0 copy-done.8
  162.8 0.3 copy.133
  163.0 1.0 copy.134
  164.0 1.5 copy.136
  165.5 1.5 copy.135
  167.1 0.7 broadcast_multiply_fusion
  167.8 45.9 %all-gather.2.cloned.1.call-done = bf16[2,2,256,768]{3,2,1,0:T(8,128)(2,1)} async-done(((bf16[2,2,16,768]{3,2,1,0:T(8,128)(2,1)}), bf16[2,2,256,768]{3,2,1,0:T(8,128)(2,1)}) %all-gather.2.cloned.1.call-update) | async-done | bytes 1572880 | tf_op jit(solution)/shard_map/all_gather | solution.py:76
  213.8 1.7 fusion.9
  215.5 1.6 fusion.1
  217.1 0.9 copy.104
  218.1 0.5 fusion.8
  218.6 0.5 fusion
  219.1 0.2 copy.101
  219.3 1.3 copy.103
  220.6 2.2 copy.106
  222.8 1.5 fusion.21
  224.3 0.5 fusion.19
  224.8 0.5 add_convert_fusion
  225.4 0.4 copy-done.4
  225.8 0.6 subtract_convert_fusion
  226.3 0.5 copy-done.2
  226.8 2.4 fusion.10
  229.2 0.6 fusion.16
  229.8 2.3 fusion.14
  232.1 2.3 fusion.12
  234.4 3.4 %copy.118 = f32[64,2,3,16,16]{0,3,4,2,1:T(8,128)} copy(f32[64,2,3,16,16]{4,3,2,1,0:T(8,128)} %fusion.10) | data formatting | bytes 786432 | tf_op jit(solution)/shard_map/qkac,kqman->kqmcn/dot_general | solution.py:102
  237.9 2.3 copy.113
  240.1 3.6 %copy.117 = f32[64,2,3,16,16]{0,3,4,2,1:T(8,128)} copy(f32[64,2,3,16,16]{4,3,2,1,0:T(8,128)} %fusion.14) | data formatting | bytes 786432 | tf_op jit(solution)/shard_map/qkac,kqman->kqmcn/dot_general | solution.py:100
  243.8 2.3 copy.114
  246.1 2.1 fusion.7
  248.1 0.2 pad_maximum_fusion.1
  248.3 1.1 copy.119
  (31 shorter events, 0.1 us)
Async XLA Ops:
  6.5 207.2 %all-gather.2.cloned.1.call-start = ((), (), s32[]{:S(2)}) async-start(), calls=%async_computation.1 | async-start | bytes 1671168 | tf_op jit(solution)/shard_map/all_gather | solution.py:76
  9.7 0.7 copy-start.10
  15.3 86.6 %copy-start.15 = (u32[256]{0:T(256)S(1)}, u32[256]{0:T(256)}, u32[]{:S(2)}) copy-start(u32[256]{0:T(256)} %constant.12) | copy-start | bytes 3076
  15.4 88.8 %copy-start.7 = (bf16[2,2,48,48]{3,2,1,0:T(8,128)(2,1)S(1)}, bf16[2,2,48,48]{3,2,1,0:T(8,128)(2,1)}, u32[]{:S(2)}) copy-start(bf16[2,2,48,48]{3,2,1,0:T(8,128)(2,1)} %param.19) | copy-start | bytes 55300
  152.7 9.9 %copy-start.12 = (s32[256,3]{0,1:T(4,128)S(1)}, s32[256,3]{0,1:T(4,128)}, u32[]{:S(2)}) copy-start(s32[256,3]{0,1:T(4,128)} %param.15) | copy-start | bytes 9220
  152.7 10.0 %copy-start.11 = (s32[64,16]{0,1:T(8,128)S(1)}, s32[64,16]{0,1:T(8,128)}, u32[]{:S(2)}) copy-start(s32[64,16]{0,1:T(8,128)} %param.22) | copy-start | bytes 12292
  152.8 10.0 %copy-start.8 = (bf16[2,64,16,16]{1,3,2,0:T(8,128)(2,1)S(1)}, bf16[2,64,16,16]{1,3,2,0:T(8,128)(2,1)}, u32[]{:S(2)}) copy-start(bf16[2,64,16,16]{1,3,2,0:T(8,128)(2,1)} %param.20) | copy-start | bytes 196612
  152.8 11.2 %copy-start.6 = (bf16[2,2,64,16,16]{2,4,3,1,0:T(8,128)(2,1)S(1)}, bf16[2,2,64,16,16]{2,4,3,1,0:T(8,128)(2,1)}, u32[]{:S(2)}) copy-start(bf16[2,2,64,16,16]{2,4,3,1,0:T(8,128)(2,1)} %param.21) | copy-start | bytes 393220
  162.6 4.4 %copy-start.14 = (s32[256]{0:T(256)S(1)}, s32[256]{0:T(256)}, u32[]{:S(2)}) copy-start(s32[256]{0:T(256)} %param.16) | copy-start | bytes 3076
  162.7 4.4 %copy-start.13 = (f32[64,3]{0,1:T(4,128)S(1)}, f32[64,3]{0,1:T(4,128)}, u32[]{:S(2)}) copy-start(f32[64,3]{0,1:T(4,128)} %param.18) | copy-start | bytes 2308
  162.7 4.5 %copy-start.9 = (s32[2,64,16]{1,2,0:T(8,128)S(1)}, s32[2,64,16]{1,2,0:T(8,128)}, u32[]{:S(2)}) copy-start(s32[2,64,16]{1,2,0:T(8,128)} %param.23) | copy-start | bytes 24580
  213.7 4.3 %copy-start.1 = (bf16[2,2,256,768]{3,2,1,0:T(8,128)(2,1)S(1)}, bf16[2,2,256,768]{3,2,1,0:T(8,128)(2,1)}, u32[]{:S(2)}) copy-start(bf16[2,2,256,768]{3,2,1,0:T(8,128)(2,1)} %all-gather.2.cloned.1.call-done) | copy-start | bytes 4718596
  224.8 1.0 copy-start.4
  225.8 1.0 copy-start.2
  226.8 2.4 copy-start.3
  240.1 3.6 %copy-start = (f32[64,2,3,16,16]{4,3,2,1,0:T(8,128)S(1)}, f32[64,2,3,16,16]{4,3,2,1,0:T(8,128)}, u32[]{:S(2)}) copy-start(f32[64,2,3,16,16]{4,3,2,1,0:T(8,128)} %fusion.12) | copy-start | bytes 1179652
  243.8 2.3 copy-start.5
Sparse Core Ops, SparseCore 0:
  162.8 50.9 all-gather.1
where the time goes:
time: 257 us; the launch traced here: 256 us
  blocking collectives  95.8 us (37%)
  local copies, waits for them, and re-layouts  74.4 us (29%)
  waiting for transfers between devices  45.9 us (18%)
  matrix products  15.8 us (6%)
  between operations  14.4 us (6%)
  other arithmetic  9.95 us (4%)
    unnamed x1, blocking collectives  86.5 us
    all_gather x1, waiting for transfers between devices, per_device(): portion = lax.all_gather(shared, 'kpt', axis=2, tiled=True)  45.9 us
    unnamed x41, local copies, waits for them, and re-layouts  34.8 us
    another operation x3, local copies, waits for them, and re-layouts, rotate_modes(): return jnp.stack([br, bi]).reshape(shape).astype(jnp.bfloat16)  10 us
    all_to_all x1, local copies, waits for them, and re-layouts, per_device(): lax.all_to_all(rotated, 'lat', split_axis=3, concat_axis=2, tiled=True)  9.89 us
    all_to_all x1, blocking collectives, per_device(): lax.all_to_all(rotated, 'lat', split_axis=3, concat_axis=2, tiled=True)  9.25 us
  transfers between devices with their start and end apart: 1, of which 1 were waited for; matrix products, arithmetic and copies ran while one was open for 2% of the time, Pallas kernels for 0%

commit v1 on v0

--- a/solution.py
+++ b/solution.py
@@ -73,7 +73,9 @@
     rotated = rotate_modes(summed, modes_rot)
     shared = lax.all_to_all(rotated, "lat", split_axis=3, concat_axis=2, tiled=True)
     lane_local = shared.shape[3]
-    portion = lax.all_gather(shared, "kpt", axis=2, tiled=True)
+    portion = jnp.concatenate(
+        lax.all_to_all(jnp.stack([shared] * lax.axis_size("kpt")), "kpt", 0, 0), axis=2
+    )
     kreal, kimag = phases(k_points, re_vectors, re_weights)
     er = jnp.einsum(
         "kr,qrx->kqx", kreal, portion[0], preferred_element_type=jnp.float32

time: 257 us -> 251 us (0.977)
  starting transfers between devices: 0.01 us -> 21.4 us
  between operations: 14.4 us -> 1.07 us
  waiting for transfers between devices: 45.9 us -> 33.2 us
    all_gather x1 -> x0, waiting for transfers between devices: 45.9 us -> none  [per_device(): portion = lax.all_gather(shared, 'kpt', axis=2, tiled=True)]
    all_to_all x0 -> x1, waiting for transfers between devices: none -> 33.2 us  [per_device(): lax.all_to_all(jnp.stack([shared] * lax.axis_size('kpt')), 'kpt', 0, 0)]
    all_to_all x0 -> x1, starting transfers between devices: none -> 21.4 us  [per_device(): lax.all_to_all(jnp.stack([shared] * lax.axis_size('kpt')), 'kpt', 0, 0)]
    another operation x2 -> x4, local copies, waits for them, and re-layouts: 1.14 us -> 11.5 us  [the longest x2 10.4 us: per_device(): jnp.stack([shared] * lax.axis_size('kpt'))]
    all_to_all x1 -> x0, local copies, waits for them, and re-layouts: 9.89 us -> none  [per_device(): lax.all_to_all(rotated, 'lat', split_axis=3, concat_axis=2, tiled=True)]
    unnamed x41 -> x39, local copies, waits for them, and re-layouts: 34.8 us -> 34.8 us
where the time goes in v1:
time: 251 us; the launch traced here: 250 us
  blocking collectives  95.8 us (38%)
  local copies, waits for them, and re-layouts  75.1 us (30%)
  waiting for transfers between devices  33.2 us (13%)
  starting transfers between devices  21.4 us (9%)
  matrix products  13.4 us (5%)
  other arithmetic  10 us (4%)
    unnamed x1, blocking collectives  86.5 us
    unnamed x39, local copies, waits for them, and re-layouts  34.8 us
    all_to_all x1, waiting for transfers between devices, per_device(): lax.all_to_all(jnp.stack([shared] * lax.axis_size('kpt')), 'kpt', 0, 0)  33.2 us
    all_to_all x1, starting transfers between devices, per_device(): lax.all_to_all(jnp.stack([shared] * lax.axis_size('kpt')), 'kpt', 0, 0)  21.4 us
    another operation x2, local copies, waits for them, and re-layouts, per_device(): jnp.stack([shared] * lax.axis_size('kpt'))  10.4 us
    another operation x3, local copies, waits for them, and re-layouts, rotate_modes(): return jnp.stack([br, bi]).reshape(shape).astype(jnp.bfloat16)  10 us
    all_to_all x1, blocking collectives, per_device(): lax.all_to_all(rotated, 'lat', split_axis=3, concat_axis=2, tiled=True)  9.25 us
  transfers between devices with their start and end apart: 1, of which 1 were waited for; matrix products, arithmetic and copies ran while one was open for 2% of the time, Pallas kernels for 0%

profile of v1, /device:TPU:1, one launch (start us, length us, event | category | flops | bytes accessed | tf_op | source)
XLA Modules:
  0.0 249.9 jit_solution(17802301658115593407)
XLA Ops:
  0.7 0.7 convert_element_type.53
  1.3 0.6 fusion.57
  1.9 1.2 convert_bitcast_fusion.1
  3.1 0.0 copy-start.9
  3.1 0.2 copy.169
  3.3 0.2 copy.170
  3.5 0.3 copy-done.9
  3.8 2.1 convert_reduce_fusion.1
  5.9 1.5 multiply_subtract_fusion
  7.4 1.4 pad_maximum_fusion
  8.9 0.0 copy-start.14
  8.9 0.0 copy-start.6
  8.9 86.5 %all-reduce.2 = bf16[2,2,16,12288]{3,1,2,0:T(2,128)(2,1)} all-reduce(f32[2,2,16,12288]{3,1,2,0:T(2,128)S(1)} %pad_maximum_fusion), channel_id=2, replica_groups=mesh['lat'=16,'kpt'=16] {'lat'}, use_global_device_ids=true, to_apply=%region_0.0.clone | all-reduce | flops 786432 | bytes 4718592
  95.4 0.6 dynamic-slice
  96.0 1.6 dynamic-slice_convert_fusion
  97.6 0.1 fusion.55
  97.7 0.2 fusion.23
  97.9 0.2 fusion.25
  98.1 0.2 fusion.4
  98.3 0.2 fusion.5
  98.5 0.1 pad_maximum_fusion.2
  98.6 10.0 %copy.129 = bf16[2,2,1,12288]{1,0,2,3:T(2,128)(2,1)} copy(bf16[2,2,1,12288]{3,1,2,0:T(2,128)(2,1)S(1)} %pad_maximum_fusion.2) | data formatting | bytes 196608 | tf_op jit(solution)/shard_map/stack | solution.py:33
  108.6 13.7 %reshape.170 = bf16[16,2,1536]{2,1,0:T(2,128)(2,1)S(1)} reshape(bf16[12288,1,2,2]{3,2,1,0:T(2,128)(2,1)} %bitcast.146) | data formatting | bytes 196608
  122.3 9.2 %all_to_all.14 = bf16[16,2,1536]{2,1,0:T(2,128)(2,1)S(1)} all-to-all(bf16[16,2,1536]{2,1,0:T(2,128)(2,1)S(1)} %reshape.170), channel_id=1, replica_groups=mesh['lat'=16,'kpt'=16] {'lat'}, dimensions={0} | all-to-all | bytes 196608 | tf_op jit(solution)/shard_map/all_to_all | solution.py:74
  131.5 14.7 %reshape.171 = bf16[12288,1,2,2]{3,2,1,0:T(2,128)(2,1)} reshape(bf16[16,2,1536]{2,1,0:T(2,128)(2,1)S(1)} %all_to_all.14) | data formatting | bytes 196608
  146.3 9.0 %copy.160 = bf16[2,2,16,768]{3,2,1,0:T(8,128)(2,1)S(1)} copy(bf16[2,2,16,768]{1,0,3,2:T(2,128)(2,1)} %bitcast.147) | data formatting | bytes 196608 | tf_op jit(solution)/shard_map/stack | solution.py:77
  155.2 1.4 stack.61
  156.6 21.4 %all-to-all-start.1 = ((bf16[16,2,2,16,768]{4,3,2,1,0:T(8,128)(2,1)}), bf16[16,2,2,16,768]{4,3,2,1,0:T(8,128)(2,1)S(1)}, u32[]{:S(2)}, u32[]{:S(2)}) async-start(bf16[16,2,2,16,768]{4,3,2,1,0:T(8,128)(2,1)} %stack.61), calls=%async_computation.1 | async-start | bytes 3145728 | tf_op jit(solution)/shard_map/all_to_all | solution.py:77
  178.0 0.0 copy-start.13
  178.0 0.0 copy-start.12
  178.1 0.3 copy.165
  178.4 1.0 copy.166
  179.4 1.5 copy.168
  180.9 1.6 copy.167
  182.5 0.7 broadcast_multiply_fusion
  183.2 33.2 %all-to-all-done.1 = bf16[16,2,2,16,768]{4,3,2,1,0:T(8,128)(2,1)S(1)} async-done(((bf16[16,2,2,16,768]{4,3,2,1,0:T(8,128)(2,1)}), bf16[16,2,2,16,768]{4,3,2,1,0:T(8,128)(2,1)S(1)}, u32[]{:S(2)}, u32[]{:S(2)}) %all-to-all-start.1) | async-done | bytes 1572896 | tf_op jit(solution)/shard_map/all_to_all | solution.py:77
  216.4 0.1 fusion.52
  216.5 0.1 copy.132
  216.6 0.1 copy.131
  216.7 0.5 fusion.44
  217.2 0.5 fusion.46
  217.7 0.5 fusion.1
  218.2 0.5 fusion
  218.7 0.9 copy.133
  219.6 0.2 copy.136
  219.8 1.3 copy.138
  221.1 2.2 copy.135
  223.3 1.5 fusion.19
  224.8 0.5 fusion.17
  225.3 0.5 add_convert_fusion
  225.9 0.4 copy-done.3
  226.3 0.5 subtract_convert_fusion
  226.8 0.5 copy-done.1
  227.3 2.3 fusion.8
  229.7 0.6 fusion.14
  230.3 2.3 fusion.12
  232.6 2.3 fusion.10
  234.9 3.5 %copy.150 = f32[64,2,3,16,16]{0,3,4,2,1:T(8,128)} copy(f32[64,2,3,16,16]{4,3,2,1,0:T(8,128)} %fusion.8) | data formatting | bytes 786432 | tf_op jit(solution)/shard_map/qkac,kqman->kqmcn/dot_general | solution.py:104
  238.3 2.3 copy.145
  240.6 3.6 %copy.149 = f32[64,2,3,16,16]{0,3,4,2,1:T(8,128)} copy(f32[64,2,3,16,16]{4,3,2,1,0:T(8,128)} %fusion.12) | data formatting | bytes 786432 | tf_op jit(solution)/shard_map/qkac,kqman->kqmcn/dot_general | solution.py:102
  244.3 2.3 copy.146
  246.5 2.1 fusion.7
  248.6 0.2 pad_maximum_fusion.1
  248.8 1.1 copy.151
  (32 shorter events, 0.1 us)
Async XLA Ops:
  3.1 0.7 copy-start.9
  8.9 86.6 %copy-start.14 = (u32[256]{0:T(256)S(1)}, u32[256]{0:T(256)}, u32[]{:S(2)}) copy-start(u32[256]{0:T(256)} %constant.12) | copy-start | bytes 3076
  8.9 88.8 %copy-start.6 = (bf16[2,2,48,48]{3,2,1,0:T(8,128)(2,1)S(1)}, bf16[2,2,48,48]{3,2,1,0:T(8,128)(2,1)}, u32[]{:S(2)}) copy-start(bf16[2,2,48,48]{3,2,1,0:T(8,128)(2,1)} %param.19) | copy-start | bytes 55300
  156.6 21.4 %copy-start.11 = (s32[256,3]{0,1:T(4,128)S(1)}, s32[256,3]{0,1:T(4,128)}, u32[]{:S(2)}) copy-start(s32[256,3]{0,1:T(4,128)} %param.15) | copy-start | bytes 9220
  156.6 21.4 %copy-start.10 = (s32[64,16]{0,1:T(8,128)S(1)}, s32[64,16]{0,1:T(8,128)}, u32[]{:S(2)}) copy-start(s32[64,16]{0,1:T(8,128)} %param.22) | copy-start | bytes 12292
  156.6 21.5 %copy-start.7 = (bf16[2,64,16,16]{1,3,2,0:T(8,128)(2,1)S(1)}, bf16[2,64,16,16]{1,3,2,0:T(8,128)(2,1)}, u32[]{:S(2)}) copy-start(bf16[2,64,16,16]{1,3,2,0:T(8,128)(2,1)} %param.20) | copy-start | bytes 196612
  156.6 22.7 %copy-start.5 = (bf16[2,2,64,16,16]{2,4,3,1,0:T(8,128)(2,1)S(1)}, bf16[2,2,64,16,16]{2,4,3,1,0:T(8,128)(2,1)}, u32[]{:S(2)}) copy-start(bf16[2,2,64,16,16]{2,4,3,1,0:T(8,128)(2,1)} %param.21) | copy-start | bytes 393220
  156.6 59.8 %all-to-all-start.1 = ((bf16[16,2,2,16,768]{4,3,2,1,0:T(8,128)(2,1)}), bf16[16,2,2,16,768]{4,3,2,1,0:T(8,128)(2,1)S(1)}, u32[]{:S(2)}, u32[]{:S(2)}) async-start(bf16[16,2,2,16,768]{4,3,2,1,0:T(8,128)(2,1)} %stack.61), calls=%async_computation.1 | async-start | bytes 3145728 | tf_op jit(solution)/shard_map/all_to_all | solution.py:77
  178.0 4.4 %copy-start.13 = (s32[256]{0:T(256)S(1)}, s32[256]{0:T(256)}, u32[]{:S(2)}) copy-start(s32[256]{0:T(256)} %param.16) | copy-start | bytes 3076
  178.0 4.4 %copy-start.12 = (f32[64,3]{0,1:T(4,128)S(1)}, f32[64,3]{0,1:T(4,128)}, u32[]{:S(2)}) copy-start(f32[64,3]{0,1:T(4,128)} %param.18) | copy-start | bytes 2308
  178.0 4.4 %copy-start.8 = (s32[2,64,16]{1,2,0:T(8,128)S(1)}, s32[2,64,16]{1,2,0:T(8,128)}, u32[]{:S(2)}) copy-start(s32[2,64,16]{1,2,0:T(8,128)} %param.23) | copy-start | bytes 24580
  225.3 1.0 copy-start.3
  226.3 1.0 copy-start.1
  227.3 2.3 copy-start.2
  240.6 3.6 %copy-start = (f32[64,2,3,16,16]{4,3,2,1,0:T(8,128)S(1)}, f32[64,2,3,16,16]{4,3,2,1,0:T(8,128)}, u32[]{:S(2)}) copy-start(f32[64,2,3,16,16]{4,3,2,1,0:T(8,128)} %fusion.10) | copy-start | bytes 1179652
  244.3 2.3 copy-start.4
